TPU v7x, 256 devices: a whole 4x4x8 slice. The times are simulated.
256 devices in a mesh: mass: 32 (over x, z), sub: 8 (over y, core).
Axes of the slice: x: 4, y: 4, z: 8, core: 2. Of those that a mesh axis runs over, the one named last changes fastest.
Arguments:
- spectra: bfloat16 [32768, 4096], P(('mass', 'sub')), may hold values from -6 to 6
- w_in: bfloat16 [4096, 2048], P(None, 'sub'), may hold values from -0.09375 to 0.09375
- w_out: bfloat16 [2048, 512], P('sub'), may hold values from -0.125 to 0.125
- partner_rows: int32 [32, 8, 32, 8], P('mass', 'sub'), may hold values from 0 to 127
- pair_counts: int32 [32, 8, 32], P('mass', 'sub'), may hold values from 0 to 8, as said below
- pair_labels: int32 [32, 8, 32, 8], P('mass', 'sub'), may hold values from 0 to 1, as said below
Outputs:
- grad_in: float32 [4096, 2048], P('mass', 'sub')
- grad_out_t: float32 [512, 2048], P('mass', 'sub')
Inputs may be any that keep to these rules, and one draw needn't show every extreme that they name: pair_counts[m, s, q] equals pair_counts[q, s, m], is 0 for q = m, and at most 8; some count equals 8. pair_labels[m, s, q, c] equals pair_labels[q, s, m, c] for q != m.
All inputs are finite; a program needn't handle non-finite values.
Results may differ from a plain program's by a relative error of at most 0.0053.
Values may be sent and summed in bfloat16 or wider, within the bound.
A program may use at most 64 MiB of HBM per device.

v0:
```python
import jax
import jax.numpy as jnp
from jax import lax
from jax.sharding import PartitionSpec as P


def per_device(spectra, w_in, w_out, partner_rows, pair_counts, pair_labels):
    own_rows = spectra.shape[0]
    peers = partner_rows.shape[2]
    slots = partner_rows.shape[3]
    shard_rows = lax.all_gather(spectra, "sub", axis=0, tiled=True)
    pre = jnp.dot(shard_rows, w_in, preferred_element_type=jnp.float32)
    hidden = jax.nn.silu(pre).astype(jnp.bfloat16)
    embed = lax.psum_scatter(
        jnp.dot(hidden, w_out, preferred_element_type=jnp.float32),
        "sub",
        scatter_dimension=0,
        tiled=True,
    )
    norm = jnp.sqrt(jnp.sum(embed * embed, axis=-1, keepdims=True) + 1e-06)
    unit = embed / norm
    unit_b = unit.astype(jnp.bfloat16)
    flat_rows = partner_rows.reshape(peers * slots)
    selector = flat_rows[:, None] == jnp.arange(own_rows, dtype=jnp.int32)[None, :]
    mine = jnp.dot(
        selector.astype(jnp.bfloat16), unit_b, preferred_element_type=jnp.float32
    ).astype(jnp.bfloat16)
    outgoing = mine.reshape(peers, slots, mine.shape[1])
    incoming = lax.all_to_all(outgoing, "mass", split_axis=0, concat_axis=0, tiled=True)
    theirs = incoming.astype(jnp.float32)
    sim = jnp.sum(outgoing.astype(jnp.float32) * theirs, axis=-1)
    valid = jnp.arange(slots, dtype=jnp.int32)[None, :] < pair_counts.reshape(peers)[:, None]
    labels = pair_labels.reshape(peers, slots).astype(jnp.float32)
    coef = jnp.where(valid, 2.0 * (sim - labels), jnp.float32(0.0))
    weighted = (coef[..., None] * theirs).reshape(peers * slots, theirs.shape[2])
    grad_unit = lax.dot_general(
        selector.astype(jnp.float32),
        weighted,
        (((0,), (0,)), ((), ())),
        precision=lax.Precision.HIGHEST,
    )
    along = jnp.sum(unit * grad_unit, axis=-1, keepdims=True)
    grad_embed = ((grad_unit - unit * along) / norm).astype(jnp.bfloat16)
    grad_rows = lax.all_gather(grad_embed, "sub", axis=0, tiled=True)
    back = lax.dot_general(
        grad_rows, w_out, (((1,), (1,)), ((), ())), preferred_element_type=jnp.float32
    )
    gate = jax.nn.sigmoid(pre)
    grad_pre = (back * gate * (1.0 + pre * (1.0 - gate))).astype(jnp.bfloat16)
    out_part = lax.dot_general(
        grad_rows, hidden, (((0,), (0,)), ((), ())), preferred_element_type=jnp.float32
    )
    in_part = lax.dot_general(
        shard_rows, grad_pre, (((0,), (0,)), ((), ())), preferred_element_type=jnp.float32
    )
    n_mass = peers
    in_rows = in_part.shape[0] // n_mass
    out_rows = out_part.shape[0] // n_mass
    partial = jnp.concatenate(
        [
            in_part.reshape(n_mass, in_rows, in_part.shape[1]),
            out_part.reshape(n_mass, out_rows, out_part.shape[1]),
        ],
        axis=1,
    ).astype(jnp.bfloat16)
    summed = jnp.sum(
        lax.all_to_all(partial, "mass", split_axis=0, concat_axis=0, tiled=True).astype(
            jnp.float32
        ),
        axis=0,
    )
    grad_in, grad_out_t = (summed[:in_rows], summed[in_rows:])
    return (grad_in, grad_out_t)


def solution(mesh):
    placed = (
        P(("mass", "sub"), None),
        P(None, "sub"),
        P("sub", None),
        P("mass", "sub", None, None),
        P("mass", "sub", None),
        P("mass", "sub", None, None),
    )
    return jax.shard_map(
        per_device,
        mesh=mesh,
        in_specs=placed,
        out_specs=(P("mass", "sub"), P("mass", "sub")),
        check_vma=False,
    )
```

profile of v0, /device:TPU:32, one launch (start us, length us, event | category | flops | bytes accessed | tf_op | source)
XLA Modules:
  0.0 248.9 jit_solution(8469015729756273993)
XLA Ops:
  7.2 0.0 copy-start
  7.2 0.0 all-gather.3.cloned.1.call-start
  7.2 0.7 all-gather.3.cloned.1.call-update
  7.9 0.0 reduce-scatter.2.cloned.1.call-start
  8.0 56.8 %all-gather.3.cloned.1.call-done = bf16[1024,4096]{1,0:T(8,128)(2,1)} async-done(((bf16[128,4096]{1,0:T(8,128)(2,1)}), bf16[1024,4096]{1,0:T(8,128)(2,1)}) %all-gather.3.cloned.1.call-update) | async-done | bytes 8388624 | tf_op jit(solution)/shard_map/all_gather | solution.py:11
  64.8 5.7 %fusion.20 = f32[1024,256]{1,0:T(8,128)S(1)} fusion(bf16[1024,4096]{1,0:T(8,128)(2,1)} %all-gather.3.cloned.1.call-done, bf16[4096,256]{1,0:T(8,128)(2,1)S(1)} %copy-done), kind=kOutput, calls=%fused_computation.37 | convolution fusion | flops 2147483648 | bytes 11534336 | tf_op jit(solution)/shard_map/dot_general | solution.py:12
  70.5 1.0 copy-done.8
  71.5 1.8 fusion.19
  73.3 0.0 reduce-scatter.2.cloned.1.call-update
  73.4 0.1 copy.13
  73.4 0.1 eq.15
  73.5 36.3 %reduce-scatter.2.cloned.1.call-done = f32[128,512]{1,0:T(8,128)} async-done(((f32[1024,512]{1,0:T(8,128)}), f32[128,512]{1,0:T(8,128)}) %reduce-scatter.2.cloned.1.call-update) | async-done | bytes 262160 | tf_op jit(solution)/shard_map/reduce_scatter | solution.py:14
  109.9 1.1 multiply_reduce_fusion.1
  111.0 2.0 fusion.3
  113.0 10.1 %all-to-all-start = ((bf16[32,8,512]{2,1,0:T(8,128)(2,1)}), bf16[32,8,512]{2,1,0:T(8,128)(2,1)S(1)}, u32[]{:S(2)}, u32[]{:S(2)}) async-start(bf16[32,8,512]{2,1,0:T(8,128)(2,1)} %fusion.3), calls=%async_computation.1 | async-start | bytes 524288 | tf_op jit(solution)/shard_map/all_to_all | solution.py:29
  123.1 0.0 all-gather.5.cloned.1.call-start
  123.1 0.1 copy.14
  123.2 10.9 %all-to-all-done = bf16[32,8,512]{2,1,0:T(8,128)(2,1)S(1)} async-done(((bf16[32,8,512]{2,1,0:T(8,128)(2,1)}), bf16[32,8,512]{2,1,0:T(8,128)(2,1)S(1)}, u32[]{:S(2)}, u32[]{:S(2)}) %all-to-all-start) | async-done | bytes 262176 | tf_op jit(solution)/shard_map/all_to_all | solution.py:29
  134.1 1.1 fusion.7
  135.2 0.1 fusion.17
  135.3 1.5 multiply_reduce_fusion
  136.8 0.8 divide_convert_fusion
  137.6 0.0 all-gather.5.cloned.1.call-update
  137.6 20.8 %all-gather.5.cloned.1.call-done = bf16[1024,512]{1,0:T(8,128)(2,1)} async-done(((bf16[128,512]{1,0:T(8,128)(2,1)}), bf16[1024,512]{1,0:T(8,128)(2,1)}) %all-gather.5.cloned.1.call-update) | async-done | bytes 1048592 | tf_op jit(solution)/shard_map/all_gather | solution.py:44
  158.4 8.6 %fusion = bf16[4096,256]{0,1:T(8,128)(2,1)} fusion(bf16[1024,4096]{1,0:T(8,128)(2,1)} %all-gather.3.cloned.1.call-done, bf16[1024,512]{1,0:T(8,128)(2,1)} %all-gather.5.cloned.1.call-done, bf16[256,512]{1,0:T(8,128)(2,1)S(1)} %copy-done.7, f32[1024,256]{1,0:T(8,128)} %copy-done.8), kind=kOutput, calls=%fused_computation.1 | convolution fusion | flops 2419326976 | bytes 12845056 | tf_op jit(solution)/shard_map/dot_general | solution.py:53
  167.0 4.2 %copy.19 = bf16[4096,256]{1,0:T(8,128)(2,1)} copy(bf16[4096,256]{0,1:T(8,128)(2,1)} %fusion) | data formatting | bytes 4194304 | tf_op jit(solution)/shard_map/reshape | solution.py:61
  171.2 1.9 convolution_convert_fusion.1
  173.1 0.2 pad_maximum_fusion
  173.3 67.5 %all_to_all.10 = bf16[32,144,256]{2,1,0:T(8,128)(2,1)S(1)} all-to-all(bf16[32,144,256]{2,1,0:T(8,128)(2,1)S(1)} %pad_maximum_fusion), channel_id=1, replica_groups=mesh['mass'=32,'sub'=8] {'mass'}, dimensions={0} | all-to-all | bytes 4718592 | tf_op jit(solution)/shard_map/all_to_all | solution.py:67
  240.8 0.3 convert_reduce_fusion
  241.1 0.6 slice.9
  241.7 0.7 slice.8
  (17 shorter events, 0.0 us)
Async XLA Ops:
  7.2 57.6 %copy-start = (bf16[4096,256]{1,0:T(8,128)(2,1)S(1)}, bf16[4096,256]{1,0:T(8,128)(2,1)}, u32[]{:S(2)}) copy-start(bf16[4096,256]{1,0:T(8,128)(2,1)} %param.7) | copy-start | bytes 6291460
  7.2 57.6 %all-gather.3.cloned.1.call-start = ((), (), s32[]{:S(2)}) async-start(), calls=%async_computation.3 | async-start | bytes 9437184 | tf_op jit(solution)/shard_map/all_gather | solution.py:11
  7.9 63.6 %copy-start.7 = (bf16[256,512]{1,0:T(8,128)(2,1)S(1)}, bf16[256,512]{1,0:T(8,128)(2,1)}, u32[]{:S(2)}) copy-start(bf16[256,512]{1,0:T(8,128)(2,1)} %param.8) | copy-start | bytes 786436
  7.9 102.0 %reduce-scatter.2.cloned.1.call-start = ((), (), s32[]{:S(2)}) async-start(), calls=%async_computation.4 | async-start | bytes 2359296 | tf_op jit(solution)/shard_map/reduce_scatter | solution.py:14
  70.5 1.0 copy-start.8
  71.5 1.9 copy-start.3
  73.3 49.8 %copy-start.4 = (s32[1,1,32,8]{2,3,1,0:T(8,128)S(1)}, s32[1,1,32,8]{2,3,1,0:T(8,128)}, u32[]{:S(2)}) copy-start(s32[1,1,32,8]{2,3,1,0:T(8,128)} %param.11) | copy-start | bytes 3076
  73.3 61.9 %copy-start.5 = (s32[1,1,32]{2,1,0:T(1,128)S(1)}, s32[1,1,32]{2,1,0:T(1,128)}, u32[]{:S(2)}) copy-start(s32[1,1,32]{2,1,0:T(1,128)} %param.10) | copy-start | bytes 388
  109.9 26.9 %copy-start.2 = (f32[128,512]{1,0:T(8,128)S(1)}, f32[128,512]{1,0:T(8,128)}, u32[]{:S(2)}) copy-start(f32[128,512]{1,0:T(8,128)} %reduce-scatter.2.cloned.1.call-done) | copy-start | bytes 786436
  113.0 21.1 %all-to-all-start = ((bf16[32,8,512]{2,1,0:T(8,128)(2,1)}), bf16[32,8,512]{2,1,0:T(8,128)(2,1)S(1)}, u32[]{:S(2)}, u32[]{:S(2)}) async-start(bf16[32,8,512]{2,1,0:T(8,128)(2,1)} %fusion.3), calls=%async_computation.1 | async-start | bytes 524288 | tf_op jit(solution)/shard_map/all_to_all | solution.py:29
  123.1 35.3 %all-gather.5.cloned.1.call-start = ((), (), s32[]{:S(2)}) async-start(), calls=%async_computation.5 | async-start | bytes 1179648 | tf_op jit(solution)/shard_map/all_gather | solution.py:44
  167.0 4.2 %copy-start.6 = (bf16[1024,512]{1,0:T(8,128)(2,1)S(1)}, bf16[1024,512]{1,0:T(8,128)(2,1)}, u32[]{:S(2)}) copy-start(bf16[1024,512]{1,0:T(8,128)(2,1)} %all-gather.5.cloned.1.call-done) | copy-start | bytes 3145732
  171.2 2.0 copy-start.1
Sparse Core Ops, SparseCore 0:
  9.9 54.8 all-gather.2
  73.5 36.3 reduce-scatter.1
  137.7 20.6 all-gather.4
where the time goes:
time: 249 us
  waiting for transfers between devices  126 us (51%)
  blocking collectives  67.5 us (27%)
  matrix products  21.5 us (9%)
  between operations  13.9 us (6%)
  starting transfers between devices  10.2 us (4%)
  local copies, waits for them, and re-layouts  6.69 us (3%)
  other arithmetic  3.58 us (1%)
    all_to_all x1, blocking collectives, per_device(): lax.all_to_all(partial, 'mass', split_axis=0, concat_axis=0, tiled=True)  67.5 us
    all_gather x1, waiting for transfers between devices, per_device(): shard_rows = lax.all_gather(spectra, 'sub', axis=0, tiled=True)  56.8 us
    reduce_scatter x1, waiting for transfers between devices, per_device(): lax.psum_scatter(jnp.dot(hidden, w_out, preferred_element_type=jnp.float3...  36.3 us
    all_gather x1, waiting for transfers between devices, per_device(): grad_rows = lax.all_gather(grad_embed, 'sub', axis=0, tiled=True)  20.8 us
    all_to_all x1, waiting for transfers between devices, per_device(): lax.all_to_all(outgoing, 'mass', split_axis=0, concat_axis=0, tiled=True)  10.9 us
    all_to_all x1, starting transfers between devices, per_device(): lax.all_to_all(outgoing, 'mass', split_axis=0, concat_axis=0, tiled=True)  10.1 us
    dot_general x1, matrix products, per_device(): lax.dot_general(shard_rows, grad_pre, (((0,), (0,)), ((), ())), preferred...  8.59 us
    dot_general x1, matrix products, per_device(): pre = jnp.dot(shard_rows, w_in, preferred_element_type=jnp.float32)  5.71 us
  transfers between devices with their start and end apart: 4, of which 4 were waited for; matrix products, arithmetic and copies ran while one was open for 0% of the time, Pallas kernels for 0%

commit v1 on v0

--- a/solution.py
+++ b/solution.py
@@ -2,6 +2,24 @@
 import jax.numpy as jnp
 from jax import lax
 from jax.sharding import PartitionSpec as P
+
+
+def gather_around(array, axis, dim):
+    ways, here, turn = (lax.axis_size(axis), lax.axis_index(axis), array.shape[dim])
+    dims = [n * ways if d == dim else n for d, n in enumerate(array.shape)]
+    full = lax.dynamic_update_slice_in_dim(
+        jnp.zeros(dims, array.dtype), array, here * turn, axis=dim
+    )
+    going_up = going_down = array
+    for far in range(1, ways // 2 + 1):
+        going_up = lax.ppermute(going_up, axis, [(d, (d + 1) % ways) for d in range(ways)])
+        full = lax.dynamic_update_slice_in_dim(full, going_up, (here - far) % ways * turn, axis=dim)
+        if 2 * far < ways:
+            going_down = lax.ppermute(going_down, axis, [(d, (d - 1) % ways) for d in range(ways)])
+            full = lax.dynamic_update_slice_in_dim(
+                full, going_down, (here + far) % ways * turn, axis=dim
+            )
+    return full
 
 
 def per_device(spectra, w_in, w_out, partner_rows, pair_counts, pair_labels):
@@ -41,7 +59,7 @@
     )
     along = jnp.sum(unit * grad_unit, axis=-1, keepdims=True)
     grad_embed = ((grad_unit - unit * along) / norm).astype(jnp.bfloat16)
-    grad_rows = lax.all_gather(grad_embed, "sub", axis=0, tiled=True)
+    grad_rows = gather_around(grad_embed, "sub", 0)
     back = lax.dot_general(
         grad_rows, w_out, (((1,), (1,)), ((), ())), preferred_element_type=jnp.float32
     )

time: 249 us -> 241 us (0.968)
  blocking collectives: 67.5 us -> 57.3 us
  starting transfers between devices: 10.2 us -> 19 us
  waiting for transfers between devices: 126 us -> 118 us
    all_gather x1 -> x0, waiting for transfers between devices: 20.8 us -> none  [per_device(): grad_rows = lax.all_gather(grad_embed, 'sub', axis=0, tiled=True)]
    ppermute x0 -> x7, waiting for transfers between devices: none -> 13.4 us  [the longest x4 13.4 us: gather_around(): lax.ppermute(going_up, axis, [(d, (d + 1) % ways) for d in range(ways)])]
    all_to_all x1, blocking collectives: 67.5 us -> 57.3 us  [per_device(): lax.all_to_all(partial, 'mass', split_axis=0, concat_axis=0, tiled=True)]
    ppermute x0 -> x7, starting transfers between devices: none -> 8.88 us  [the longest x3 8.85 us: gather_around(): lax.ppermute(going_down, axis, [(d, (d - 1) % ways) for d in range(ways)])]
  transfers between devices with their start and end apart: 4 -> 10, of which waited for: 4 -> 7; matrix products, arithmetic and copies ran while one was open for 0% -> 0% of each run, Pallas kernels for 0% -> 0%
where the time goes in v1:
time: 241 us; the launch traced here: 240 us
  waiting for transfers between devices  118 us (49%)
  blocking collectives  57.3 us (24%)
  matrix products  21.2 us (9%)
  starting transfers between devices  19 us (8%)
  between operations  14.2 us (6%)
  local copies, waits for them, and re-layouts  5.79 us (2%)
  other arithmetic  4.51 us (2%)
    all_to_all x1, blocking collectives, per_device(): lax.all_to_all(partial, 'mass', split_axis=0, concat_axis=0, tiled=True)  57.3 us
    all_gather x1, waiting for transfers between devices, per_device(): shard_rows = lax.all_gather(spectra, 'sub', axis=0, tiled=True)  56.8 us
    reduce_scatter x1, waiting for transfers between devices, per_device(): lax.psum_scatter(jnp.dot(hidden, w_out, preferred_element_type=jnp.float3...  36.3 us
    ppermute x4, waiting for transfers between devices, gather_around(): lax.ppermute(going_up, axis, [(d, (d + 1) % ways) for d in range(ways)])  13.4 us
    all_to_all x1, waiting for transfers between devices, per_device(): lax.all_to_all(outgoing, 'mass', split_axis=0, concat_axis=0, tiled=True)  11 us
    all_to_all x1, starting transfers between devices, per_device(): lax.all_to_all(outgoing, 'mass', split_axis=0, concat_axis=0, tiled=True)  10 us
    ppermute x3, starting transfers between devices, gather_around(): lax.ppermute(going_down, axis, [(d, (d - 1) % ways) for d in range(ways)])  8.85 us
    dot_general x1, matrix products, per_device(): lax.dot_general(shard_rows, grad_pre, (((0,), (0,)), ((), ())), preferred...  8.36 us
  transfers between devices with their start and end apart: 10, of which 7 were waited for; matrix products, arithmetic and copies ran while one was open for 0% of the time, Pallas kernels for 0%

profile of v1, /device:TPU:32, one launch (start us, length us, event | category | flops | bytes accessed | tf_op | source)
XLA Modules:
  0.0 240.3 jit_solution(198959262908838978)
XLA Ops:
  7.2 0.7 all-gather.2.cloned.1.call-update
  8.0 56.8 %all-gather.2.cloned.1.call-done = bf16[1024,4096]{1,0:T(8,128)(2,1)} async-done(((bf16[128,4096]{1,0:T(8,128)(2,1)}), bf16[1024,4096]{1,0:T(8,128)(2,1)}) %all-gather.2.cloned.1.call-update) | async-done | bytes 8388624 | tf_op jit(solution)/shard_map/all_gather | solution.py:29
  64.8 5.7 %fusion.20 = f32[1024,256]{1,0:T(8,128)S(1)} fusion(bf16[1024,4096]{1,0:T(8,128)(2,1)} %all-gather.2.cloned.1.call-done, bf16[4096,256]{1,0:T(8,128)(2,1)S(1)} %copy-done), kind=kOutput, calls=%fused_computation.45 | convolution fusion | flops 2147483648 | bytes 11534336 | tf_op jit(solution)/shard_map/dot_general | solution.py:30
  70.6 1.8 fusion.19
  72.4 0.1 copy.13
  72.5 0.1 eq.23
  72.6 36.3 %reduce-scatter.2.cloned.1.call-done = f32[128,512]{1,0:T(8,128)} async-done(((f32[1024,512]{1,0:T(8,128)}), f32[128,512]{1,0:T(8,128)}) %reduce-scatter.2.cloned.1.call-update) | async-done | bytes 262160 | tf_op jit(solution)/shard_map/reduce_scatter | solution.py:32
  108.9 1.1 multiply_reduce_fusion.1
  110.1 2.0 fusion.3
  112.1 10.0 %all-to-all-start = ((bf16[32,8,512]{2,1,0:T(8,128)(2,1)}), bf16[32,8,512]{2,1,0:T(8,128)(2,1)S(1)}, u32[]{:S(2)}, u32[]{:S(2)}) async-start(bf16[32,8,512]{2,1,0:T(8,128)(2,1)} %fusion.3), calls=%async_computation.1 | async-start | bytes 524288 | tf_op jit(solution)/shard_map/all_to_all | solution.py:47
  122.1 0.1 copy.14
  122.2 11.0 %all-to-all-done = bf16[32,8,512]{2,1,0:T(8,128)(2,1)S(1)} async-done(((bf16[32,8,512]{2,1,0:T(8,128)(2,1)}), bf16[32,8,512]{2,1,0:T(8,128)(2,1)S(1)}, u32[]{:S(2)}, u32[]{:S(2)}) %all-to-all-start) | async-done | bytes 262176 | tf_op jit(solution)/shard_map/all_to_all | solution.py:47
  133.2 1.1 fusion.7
  134.3 0.1 fusion.17
  134.3 1.5 multiply_reduce_fusion
  135.8 0.1 broadcast_in_dim.6
  135.9 0.1 constant_dynamic-update-slice_fusion.7
  136.1 2.9 %collective-permute-start.1 = (bf16[128,512]{1,0:T(8,128)(2,1)S(1)}, bf16[128,512]{1,0:T(8,128)(2,1)S(1)}, u32[]{:S(2)}, u32[]{:S(2)}) collective-permute-start(bf16[128,512]{1,0:T(8,128)(2,1)S(1)} %get-tuple-element.5), channel_id=1, source_target_pairs={{0,7},{1,0},{2,1},{3,2},{4,3},{5,4},{6,5},{7,6},{8,15},{9,8},{10,9... | collective-permute-start | bytes 393224 | tf_op jit(solution)/shard_map/ppermute | solution.py:18
  139.0 2.6 %collective-permute-done = bf16[128,512]{1,0:T(8,128)(2,1)S(1)} collective-permute-done((bf16[128,512]{1,0:T(8,128)(2,1)S(1)}, bf16[128,512]{1,0:T(8,128)(2,1)S(1)}, u32[]{:S(2)}, u32[]{:S(2)}) %collective-permute-start) | collective-permute-done | bytes 131104 | tf_op jit(solution)/shard_map/ppermute | solution.py:15
  141.7 3.0 %collective-permute-start.3 = (bf16[128,512]{1,0:T(8,128)(2,1)S(1)}, bf16[128,512]{1,0:T(8,128)(2,1)S(1)}, u32[]{:S(2)}, u32[]{:S(2)}) collective-permute-start(bf16[128,512]{1,0:T(8,128)(2,1)S(1)} %collective-permute-done.1), channel_id=1, source_target_pairs={{0,7},{1,0},{2,1},{3,2},{4,3},{5,4},{6,5},{7,6},{8,15},{9,8},{10,9... | collective-permute-start | bytes 393224 | tf_op jit(solution)/shard_map/ppermute | solution.py:18
  144.7 2.6 %collective-permute-done.2 = bf16[128,512]{1,0:T(8,128)(2,1)S(1)} collective-permute-done((bf16[128,512]{1,0:T(8,128)(2,1)S(1)}, bf16[128,512]{1,0:T(8,128)(2,1)S(1)}, u32[]{:S(2)}, u32[]{:S(2)}) %collective-permute-start.2) | collective-permute-done | bytes 131104 | tf_op jit(solution)/shard_map/ppermute | solution.py:15
  147.3 3.0 %collective-permute-start.5 = (bf16[128,512]{1,0:T(8,128)(2,1)S(1)}, bf16[128,512]{1,0:T(8,128)(2,1)S(1)}, u32[]{:S(2)}, u32[]{:S(2)}) collective-permute-start(bf16[128,512]{1,0:T(8,128)(2,1)S(1)} %collective-permute-done.3), channel_id=1, source_target_pairs={{0,7},{1,0},{2,1},{3,2},{4,3},{5,4},{6,5},{7,6},{8,15},{9,8},{10,9... | collective-permute-start | bytes 393224 | tf_op jit(solution)/shard_map/ppermute | solution.py:18
  150.3 2.6 %collective-permute-done.4 = bf16[128,512]{1,0:T(8,128)(2,1)S(1)} collective-permute-done((bf16[128,512]{1,0:T(8,128)(2,1)S(1)}, bf16[128,512]{1,0:T(8,128)(2,1)S(1)}, u32[]{:S(2)}, u32[]{:S(2)}) %collective-permute-start.4) | collective-permute-done | bytes 131104 | tf_op jit(solution)/shard_map/ppermute | solution.py:15
  152.9 5.5 %collective-permute-done.6 = bf16[128,512]{1,0:T(8,128)(2,1)S(1)} collective-permute-done((bf16[128,512]{1,0:T(8,128)(2,1)S(1)}, bf16[128,512]{1,0:T(8,128)(2,1)S(1)}, u32[]{:S(2)}, u32[]{:S(2)}) %collective-permute-start.6) | collective-permute-done | bytes 131104 | tf_op jit(solution)/shard_map/ppermute | solution.py:15
  158.5 1.8 convolution_convert_fusion.1
  160.3 8.4 %fusion = bf16[4096,256]{0,1:T(8,128)(2,1)} fusion(bf16[1024,4096]{1,0:T(8,128)(2,1)} %all-gather.2.cloned.1.call-done, bf16[1024,512]{1,0:T(8,128)(2,1)S(1)} %constant_dynamic-update-slice_fusion, bf16[256,512]{1,0:T(8,128)(2,1)} %param.8, f32[1024,256]{1,0:T(8,128)} %copy-done.6), kind=kOutput, calls=%fused_computation.1 | convolution fusion | flops 2419326976 | bytes 12845056 | tf_op jit(solution)/shard_map/dot_general | solution.py:71
  168.6 4.1 %copy.19 = bf16[4096,256]{1,0:T(8,128)(2,1)} copy(bf16[4096,256]{0,1:T(8,128)(2,1)} %fusion) | data formatting | bytes 4194304 | tf_op jit(solution)/shard_map/reshape | solution.py:79
  172.7 1.8 pad_maximum_fusion
  174.5 57.3 %all_to_all.10 = bf16[32,144,256]{2,1,0:T(8,128)(2,1)S(1)} all-to-all(bf16[32,144,256]{2,1,0:T(8,128)(2,1)S(1)} %pad_maximum_fusion), channel_id=1, replica_groups=mesh['mass'=32,'sub'=8] {'mass'}, dimensions={0} | all-to-all | bytes 4718592 | tf_op jit(solution)/shard_map/all_to_all | solution.py:85
  231.8 0.3 convert_reduce_fusion
  232.2 0.7 slice.8
  232.8 0.6 slice.9
  (32 shorter events, 0.3 us)
Async XLA Ops:
  7.2 57.6 %copy-start = (bf16[4096,256]{1,0:T(8,128)(2,1)S(1)}, bf16[4096,256]{1,0:T(8,128)(2,1)}, u32[]{:S(2)}) copy-start(bf16[4096,256]{1,0:T(8,128)(2,1)} %param.7) | copy-start | bytes 6291460
  7.2 57.6 %all-gather.2.cloned.1.call-start = ((), (), s32[]{:S(2)}) async-start(), calls=%async_computation.3 | async-start | bytes 9437184 | tf_op jit(solution)/shard_map/all_gather | solution.py:29
  7.9 62.6 %copy-start.5 = (bf16[256,512]{1,0:T(8,128)(2,1)S(1)}, bf16[256,512]{1,0:T(8,128)(2,1)}, u32[]{:S(2)}) copy-start(bf16[256,512]{1,0:T(8,128)(2,1)} %param.8) | copy-start | bytes 786436
  7.9 101.0 %reduce-scatter.2.cloned.1.call-start = ((), (), s32[]{:S(2)}) async-start(), calls=%async_computation.4 | async-start | bytes 2359296 | tf_op jit(solution)/shard_map/reduce_scatter | solution.py:32
  70.5 1.9 copy-start.6
  70.6 1.9 copy-start.2
  72.4 49.7 %copy-start.3 = (s32[1,1,32,8]{2,3,1,0:T(8,128)S(1)}, s32[1,1,32,8]{2,3,1,0:T(8,128)}, u32[]{:S(2)}) copy-start(s32[1,1,32,8]{2,3,1,0:T(8,128)} %param.11) | copy-start | bytes 3076
  72.4 61.9 %copy-start.4 = (s32[1,1,32]{2,1,0:T(1,128)S(1)}, s32[1,1,32]{2,1,0:T(1,128)}, u32[]{:S(2)}) copy-start(s32[1,1,32]{2,1,0:T(1,128)} %param.10) | copy-start | bytes 388
  108.9 27.0 %copy-start.1 = (f32[128,512]{1,0:T(8,128)S(1)}, f32[128,512]{1,0:T(8,128)}, u32[]{:S(2)}) copy-start(f32[128,512]{1,0:T(8,128)} %reduce-scatter.2.cloned.1.call-done) | copy-start | bytes 786436
  112.1 21.1 %all-to-all-start = ((bf16[32,8,512]{2,1,0:T(8,128)(2,1)}), bf16[32,8,512]{2,1,0:T(8,128)(2,1)S(1)}, u32[]{:S(2)}, u32[]{:S(2)}) async-start(bf16[32,8,512]{2,1,0:T(8,128)(2,1)} %fusion.3), calls=%async_computation.1 | async-start | bytes 524288 | tf_op jit(solution)/shard_map/all_to_all | solution.py:47
  136.0 5.6 %collective-permute-start = (bf16[128,512]{1,0:T(8,128)(2,1)S(1)}, bf16[128,512]{1,0:T(8,128)(2,1)S(1)}, u32[]{:S(2)}, u32[]{:S(2)}) collective-permute-start(bf16[128,512]{1,0:T(8,128)(2,1)S(1)} %get-tuple-element.5), channel_id=1, source_target_pairs={{0,1},{1,2},{2,3},{3,4},{4,5},{5,6},{6,7},{7,0},{8,9},{9,10},{10,1... | collective-permute-start | bytes 393224 | tf_op jit(solution)/shard_map/ppermute | solution.py:15
  136.1 5.6 %collective-permute-start.1 = (bf16[128,512]{1,0:T(8,128)(2,1)S(1)}, bf16[128,512]{1,0:T(8,128)(2,1)S(1)}, u32[]{:S(2)}, u32[]{:S(2)}) collective-permute-start(bf16[128,512]{1,0:T(8,128)(2,1)S(1)} %get-tuple-element.5), channel_id=1, source_target_pairs={{0,7},{1,0},{2,1},{3,2},{4,3},{5,4},{6,5},{7,6},{8,15},{9,8},{10,9... | collective-permute-start | bytes 393224 | tf_op jit(solution)/shard_map/ppermute | solution.py:18
  141.7 5.6 %collective-permute-start.2 = (bf16[128,512]{1,0:T(8,128)(2,1)S(1)}, bf16[128,512]{1,0:T(8,128)(2,1)S(1)}, u32[]{:S(2)}, u32[]{:S(2)}) collective-permute-start(bf16[128,512]{1,0:T(8,128)(2,1)S(1)} %collective-permute-done), channel_id=1, source_target_pairs={{0,1},{1,2},{2,3},{3,4},{4,5},{5,6},{6,7},{7,0},{8,9},{9,10},{10,1... | collective-permute-start | bytes 393224 | tf_op jit(solution)/shard_map/ppermute | solution.py:15
  141.7 5.6 %collective-permute-start.3 = (bf16[128,512]{1,0:T(8,128)(2,1)S(1)}, bf16[128,512]{1,0:T(8,128)(2,1)S(1)}, u32[]{:S(2)}, u32[]{:S(2)}) collective-permute-start(bf16[128,512]{1,0:T(8,128)(2,1)S(1)} %collective-permute-done.1), channel_id=1, source_target_pairs={{0,7},{1,0},{2,1},{3,2},{4,3},{5,4},{6,5},{7,6},{8,15},{9,8},{10,9... | collective-permute-start | bytes 393224 | tf_op jit(solution)/shard_map/ppermute | solution.py:18
  147.3 5.6 %collective-permute-start.4 = (bf16[128,512]{1,0:T(8,128)(2,1)S(1)}, bf16[128,512]{1,0:T(8,128)(2,1)S(1)}, u32[]{:S(2)}, u32[]{:S(2)}) collective-permute-start(bf16[128,512]{1,0:T(8,128)(2,1)S(1)} %collective-permute-done.2), channel_id=1, source_target_pairs={{0,1},{1,2},{2,3},{3,4},{4,5},{5,6},{6,7},{7,0},{8,9},{9,10},{10,1... | collective-permute-start | bytes 393224 | tf_op jit(solution)/shard_map/ppermute | solution.py:15
  147.3 5.6 %collective-permute-start.5 = (bf16[128,512]{1,0:T(8,128)(2,1)S(1)}, bf16[128,512]{1,0:T(8,128)(2,1)S(1)}, u32[]{:S(2)}, u32[]{:S(2)}) collective-permute-start(bf16[128,512]{1,0:T(8,128)(2,1)S(1)} %collective-permute-done.3), channel_id=1, source_target_pairs={{0,7},{1,0},{2,1},{3,2},{4,3},{5,4},{6,5},{7,6},{8,15},{9,8},{10,9... | collective-permute-start | bytes 393224 | tf_op jit(solution)/shard_map/ppermute | solution.py:18
  152.9 5.6 %collective-permute-start.6 = (bf16[128,512]{1,0:T(8,128)(2,1)S(1)}, bf16[128,512]{1,0:T(8,128)(2,1)S(1)}, u32[]{:S(2)}, u32[]{:S(2)}) collective-permute-start(bf16[128,512]{1,0:T(8,128)(2,1)S(1)} %collective-permute-done.4), channel_id=1, source_target_pairs={{0,1},{1,2},{2,3},{3,4},{4,5},{5,6},{6,7},{7,0},{8,9},{9,10},{10,1... | collective-permute-start | bytes 393224 | tf_op jit(solution)/shard_map/ppermute | solution.py:15
Sparse Core Ops, SparseCore 0:
  9.9 54.8 all-gather.1
  72.5 36.3 reduce-scatter.1
